TPU v7x, 32 devices: a whole 2x2x4 slice. The times are simulated.
32 devices in a mesh: tiles: 2 (over x), space: 8 (over z, y), chan: 2 (over core).
Axes of the slice: x: 2, y: 2, z: 4, core: 2. Of those that a mesh axis runs over, the one named last changes fastest.
Arguments:
- volume: bfloat16 [32, 64, 32, 256], P(None, 'space', 'tiles', 'chan'), parts along dimension 2, may hold values from -6 to 6
- weight_one: bfloat16 [3, 3, 3, 256, 256], replicated, may hold values from -0.078125 to 0.078125
- bias_one: float32 [256], replicated, may hold values from -3 to 3
- weight_two: bfloat16 [3, 3, 3, 256, 256], replicated, may hold values from -0.078125 to 0.078125
- bias_two: float32 [256], replicated, may hold values from -3 to 3
Outputs:
- features: bfloat16 [32, 64, 32, 256], P('space', None, 'tiles', 'chan'), parts along dimension 2
There are 2 independent parts, one for each index of `tiles`. A program takes and returns all parts, laid end to end along the dimension named above; an argument that names none is the same for every part. Nothing has to cross between parts.
All inputs are finite; a program needn't handle non-finite values.
Results may differ from a plain program's by a relative error of at most 0.0044.
Values may be sent and summed in bfloat16 or wider, within the bound.
A program may use at most 128 MiB of HBM per device.

v0:
```python
import jax
import jax.numpy as jnp
from jax import lax
from jax.sharding import PartitionSpec as P


def padded(x, sides, width):
    for axis, dim in sides:
        devices, length = (lax.axis_size(axis), x.shape[dim])
        up = [(i, (i + 1) % devices) for i in range(devices - 1)]
        down = [(j, i) for i, j in up]
        last = lax.slice_in_dim(x, length - width, length, axis=dim)
        first = lax.slice_in_dim(x, 0, width, axis=dim)
        before = lax.ppermute(last, axis, up)
        after = lax.ppermute(first, axis, down)
        x = jnp.concatenate([before, x, after], axis=dim)
    return x


def convolve(field, kernel):
    return lax.conv_general_dilated(
        field[None],
        kernel,
        (1, 1, 1),
        ((0, 0), (1, 1), (1, 1)),
        dimension_numbers=("NDHWC", "DHWIO", "NDHWC"),
        preferred_element_type=jnp.float32,
    )[0]


def pad_layer(field):
    return padded(field, (("space", 0),), 1)


def body(volume, weight_one, bias_one, weight_two, bias_two):
    slab_data = lax.all_to_all(volume, "space", split_axis=0, concat_axis=1, tiled=True)
    share = slab_data.shape[3]
    offset = lax.axis_index("chan") * share

    def layer(field, kernel, bias):
        part_kernel = lax.dynamic_slice_in_dim(kernel, offset, share, 3)
        summed = lax.psum_scatter(
            convolve(field, part_kernel), "chan", scatter_dimension=3, tiled=True
        )
        return summed + lax.dynamic_slice_in_dim(bias, offset, share, 0)

    hidden = jnp.maximum(layer(pad_layer(slab_data), weight_one, bias_one), 0.0).astype(
        jnp.bfloat16
    )
    result = layer(pad_layer(hidden), weight_two, bias_two)
    return jnp.maximum(result, 0.0).astype(jnp.bfloat16)


def solution(mesh):
    return jax.shard_map(
        body,
        mesh=mesh,
        in_specs=(P(None, "space", "tiles", "chan"), P(), P(), P(), P()),
        out_specs=P("space", None, "tiles", "chan"),
        check_vma=False,
    )
```

profile of v0, /device:TPU:1, one launch (start us, length us, event | category | flops | bytes accessed | tf_op | source)
XLA Modules:
  0.0 152.1 jit_solution(18392344283605213715)
XLA Ops:
  6.5 0.0 copy-start
  6.5 0.0 reduce-scatter.3.cloned.1.call-start
  6.5 31.6 %all_to_all.18 = bf16[32,8,16,128]{3,2,1,0:T(8,128)(2,1)S(1)} all-to-all(bf16[32,8,16,128]{3,2,1,0:T(8,128)(2,1)} %param.5), channel_id=1, replica_groups=mesh['tiles'=2,'space'=8,'chan'=2] {'space'}, dimensions={0} | all-to-all | bytes 2097152 | tf_op jit(solution)/shard_map/all_to_all | solution.py:36
  38.1 0.0 copy-start.2
  38.1 1.0 copy-done.2
  39.1 0.8 fusion.33
  39.9 3.8 %collective-permute-start = (bf16[1,64,16,128]{3,2,1,0:T(8,128)(2,1)}, bf16[1,64,16,128]{3,2,1,0:T(8,128)(2,1)}, u32[]{:S(2)}, u32[]{:S(2)}) collective-permute-start(bf16[1,64,16,128]{3,2,1,0:T(8,128)(2,1)} %bitcast.2), channel_id=1, source_target_pairs={{0,2},{2,4},{4,6},{6,8},{8,10},{10,12},{12,14},{1,3},{3,5},{5,7},{... | collective-permute-start | bytes 786440 | tf_op jit(solution)/shard_map/ppermute | solution.py:14
  43.7 1.3 collective-permute-start.1
  45.0 1.4 copy.14
  46.4 0.7 collective-permute-done
  47.1 4.5 %collective-permute-done.1 = bf16[1,64,16,128]{3,2,1,0:T(8,128)(2,1)} collective-permute-done((bf16[1,64,16,128]{3,2,1,0:T(8,128)(2,1)}, bf16[1,64,16,128]{3,2,1,0:T(8,128)(2,1)}, u32[]{:S(2)}, u32[]{:S(2)}) %collective-permute-start.1) | collective-permute-done | bytes 262176 | tf_op jit(solution)/shard_map/ppermute | solution.py:15
  51.6 1.2 maximum_bitcast_fusion
  52.8 0.4 copy.23
  53.2 0.4 pad.clone
  53.6 1.5 %copy.17 = bf16[6,64,1,8,3,128]{5,3,4,1,0,2:T(8,128)(2,1)S(1)} copy(bf16[6,64,1,8,3,128]{5,1,4,3,0,2:T(8,128)(2,1)S(1)} %bitcast.31) | data formatting | bytes 4718592 | tf_op jit(solution)/shard_map/conv_general_dilated | solution.py:21
  55.2 0.0 copy-start.6
  55.2 0.4 slice.30
  55.6 0.0 copy-done
  55.6 0.2 copy-done.6
  55.8 13.5 %broadcast_select_fusion.1 = f32[4,64,8,3,256]{4,2,3,1,0:T(8,128)S(1)} fusion(pred[8,3]{0,1:T(4,128)(4,1)S(1)} %copy-done.6, bf16[6,64,1,7,2,128]{5,3,4,1,0,2:T(8,128)(2,1)S(1)} %slice.30, bf16[6,64,1,8,3,128]{5,3,4,1,0,2:T(8,128)(2,1)S(1)} %copy.17, bf16[3,3,3,256,256]{4,3,2,1,0:T(8,128)(2,1)S(1)} %copy-done, s32[]{:T(128)S(6)} %select_n.2), kind=kOutput, calls=%fused_computation.18 | convolution fusion | flops 10771759104 | bytes 11993604 | tf_op jit(solution)/shard_map/conv_general_dilated | solution.py:21
  69.3 1.9 %copy.18 = f32[4,64,8,3,256]{4,1,3,2,0:T(8,128)S(1)} copy(f32[4,64,8,3,256]{4,2,3,1,0:T(8,128)S(1)} %broadcast_select_fusion.1) | data formatting | bytes 12582912 | tf_op jit(solution)/shard_map/conv_general_dilated | solution.py:21
  71.2 2.4 %slice_bitcast_fusion.1 = f32[4,64,16,256]{3,1,2,0:T(8,128)} fusion(f32[4,64,1,24,256]{4,1,3,0,2:T(8,128)S(1)} %bitcast.28), kind=kLoop, calls=%fused_computation.4 | loop fusion | bytes 8388608 | tf_op jit(solution)/shard_map/squeeze | solution.py:21
  73.7 0.0 reduce-scatter.3.cloned.1.call-update
  73.7 0.0 reduce-scatter.5.cloned.1.call-start
  73.7 0.6 copy-done.4
  74.3 0.1 dynamic_slice.13
  74.4 15.5 %reduce-scatter.3.cloned.1.call-done = f32[4,64,16,128]{3,1,2,0:T(8,128)} async-done(((f32[4,64,16,256]{3,1,2,0:T(8,128)}), f32[4,64,16,128]{3,1,2,0:T(8,128)}) %reduce-scatter.3.cloned.1.call-update) | async-done | bytes 2097168 | tf_op jit(solution)/shard_map/reduce_scatter | solution.py:42
  89.9 1.9 %maximum_convert_fusion.1 = bf16[4,64,16,128]{3,1,2,0:T(8,128)(2,1)S(1)} fusion(f32[4,64,16,128]{3,1,2,0:T(8,128)} %reduce-scatter.3.cloned.1.call-done, f32[128]{0:T(128)S(1)} %dynamic_slice.13), kind=kLoop, calls=%fused_computation.20 | loop fusion | flops 1572864 | bytes 3146240 | tf_op jit(solution)/shard_map/convert_element_type | solution.py:47
  91.9 3.4 %collective-permute-start.2 = (bf16[1,64,16,128]{3,1,2,0:T(8,128)(2,1)S(1)}, bf16[1,64,16,128]{3,1,2,0:T(8,128)(2,1)S(1)}, u32[]{:S(2)}, u32[]{:S(2)}) collective-permute-start(bf16[1,64,16,128]{3,1,2,0:T(8,128)(2,1)S(1)} %get-tuple-element.5), channel_id=1, source_target_pairs={{0,2},{2,4},{4,6},{6,8},{8,10},{10,12},{12,14},{1,3},{3,5},{5,7},{... | collective-permute-start | bytes 786440 | tf_op jit(solution)/shard_map/ppermute | solution.py:14
  95.2 1.5 collective-permute-start.3
  96.7 9.3 %collective-permute-done.2 = bf16[1,64,16,128]{3,1,2,0:T(8,128)(2,1)S(1)} collective-permute-done((bf16[1,64,16,128]{3,1,2,0:T(8,128)(2,1)S(1)}, bf16[1,64,16,128]{3,1,2,0:T(8,128)(2,1)S(1)}, u32[]{:S(2)}, u32[]{:S(2)}) %collective-permute-start.2) | collective-permute-done | bytes 262176 | tf_op jit(solution)/shard_map/ppermute | solution.py:14
  106.1 0.0 collective-permute-done.3
  106.1 0.2 maximum_bitcast_fusion.1
  106.2 0.4 pad.2
  106.6 0.0 copy-start.3
  106.6 1.5 %copy.20 = bf16[6,64,1,8,3,128]{5,3,4,1,0,2:T(8,128)(2,1)S(1)} copy(bf16[6,64,1,8,3,128]{5,1,4,3,0,2:T(8,128)(2,1)S(1)} %bitcast.30) | data formatting | bytes 4718592 | tf_op jit(solution)/shard_map/conv_general_dilated | solution.py:21
  108.2 0.4 slice.34
  108.6 0.0 copy-done.3
  108.6 13.5 %broadcast_select_fusion = f32[4,64,8,3,256]{4,2,3,1,0:T(8,128)S(1)} fusion(pred[8,3]{0,1:T(4,128)(4,1)S(1)} %copy-done.6, bf16[6,64,1,7,2,128]{5,3,4,1,0,2:T(8,128)(2,1)S(1)} %slice.34, bf16[6,64,1,8,3,128]{5,3,4,1,0,2:T(8,128)(2,1)S(1)} %copy.20, bf16[3,3,3,256,256]{4,3,2,1,0:T(8,128)(2,1)S(1)} %copy-done.3, s32[]{:T(128)S(6)} %select_n.2), kind=kOutput, calls=%fused_computation.17 | convolution fusion | flops 10771759104 | bytes 11993604 | tf_op jit(solution)/shard_map/conv_general_dilated | solution.py:21
  122.1 1.9 %copy.21 = f32[4,64,8,3,256]{4,1,3,2,0:T(8,128)S(1)} copy(f32[4,64,8,3,256]{4,2,3,1,0:T(8,128)S(1)} %broadcast_select_fusion) | data formatting | bytes 12582912 | tf_op jit(solution)/shard_map/conv_general_dilated | solution.py:21
  124.1 2.4 %slice_bitcast_fusion = f32[4,64,16,256]{3,1,2,0:T(8,128)} fusion(f32[4,64,1,24,256]{4,1,3,0,2:T(8,128)S(1)} %bitcast.29), kind=kLoop, calls=%fused_computation.3 | loop fusion | bytes 8388608 | tf_op jit(solution)/shard_map/squeeze | solution.py:21
  126.5 0.0 reduce-scatter.5.cloned.1.call-update
  126.5 0.7 copy-done.5
  127.2 0.1 dynamic_slice.15
  127.3 14.5 %reduce-scatter.5.cloned.1.call-done = f32[4,64,16,128]{3,1,2,0:T(8,128)} async-done(((f32[4,64,16,256]{3,1,2,0:T(8,128)}), f32[4,64,16,128]{3,1,2,0:T(8,128)}) %reduce-scatter.5.cloned.1.call-update) | async-done | bytes 2097168 | tf_op jit(solution)/shard_map/reduce_scatter | solution.py:42
  141.7 1.9 %maximum_convert_fusion = bf16[4,64,16,128]{3,1,2,0:T(8,128)(2,1)S(1)} fusion(f32[4,64,16,128]{3,1,2,0:T(8,128)} %reduce-scatter.5.cloned.1.call-done, f32[128]{0:T(128)S(1)} %dynamic_slice.15), kind=kLoop, calls=%fused_computation.19 | loop fusion | flops 1572864 | bytes 3146240 | tf_op jit(solution)/shard_map/convert_element_type | solution.py:51
  143.6 1.7 %copy.22 = bf16[4,64,16,128]{3,2,1,0:T(8,128)(2,1)} copy(bf16[4,64,16,128]{3,1,2,0:T(8,128)(2,1)S(1)} %maximum_convert_fusion) | data formatting | bytes 2097152 | tf_op jit(solution)/shard_map/convert_element_type | solution.py:51
  145.3 0.0 copy-done.1
  (4 shorter events, 0.0 us)
Async XLA Ops:
  6.5 49.1 %copy-start = (bf16[3,3,3,256,256]{4,3,2,1,0:T(8,128)(2,1)S(1)}, bf16[3,3,3,256,256]{4,3,2,1,0:T(8,128)(2,1)}, u32[]{:S(2)}) copy-start(bf16[3,3,3,256,256]{4,3,2,1,0:T(8,128)(2,1)} %param.6) | copy-start | bytes 10616836
  6.5 83.4 %reduce-scatter.3.cloned.1.call-start = ((), (), s32[]{:S(2)}) async-start(), calls=%async_computation.3 | async-start | bytes 6291456 | tf_op jit(solution)/shard_map/reduce_scatter | solution.py:42
  38.1 1.0 copy-start.2
  39.9 7.2 %collective-permute-start = (bf16[1,64,16,128]{3,2,1,0:T(8,128)(2,1)}, bf16[1,64,16,128]{3,2,1,0:T(8,128)(2,1)}, u32[]{:S(2)}, u32[]{:S(2)}) collective-permute-start(bf16[1,64,16,128]{3,2,1,0:T(8,128)(2,1)} %bitcast.2), channel_id=1, source_target_pairs={{0,2},{2,4},{4,6},{6,8},{8,10},{10,12},{12,14},{1,3},{3,5},{5,7},{... | collective-permute-start | bytes 786440 | tf_op jit(solution)/shard_map/ppermute | solution.py:14
  43.7 7.9 %collective-permute-start.1 = (bf16[1,64,16,128]{3,2,1,0:T(8,128)(2,1)}, bf16[1,64,16,128]{3,2,1,0:T(8,128)(2,1)}, u32[]{:S(2)}, u32[]{:S(2)}) collective-permute-start(bf16[1,64,16,128]{3,2,1,0:T(8,128)(2,1)} %bitcast.5), channel_id=1, source_target_pairs={{2,0},{4,2},{6,4},{8,6},{10,8},{12,10},{14,12},{3,1},{5,3},{7,5},{... | collective-permute-start | bytes 786440 | tf_op jit(solution)/shard_map/ppermute | solution.py:15
  55.2 0.7 copy-start.6
  73.7 0.7 copy-start.4
  73.7 68.1 %reduce-scatter.5.cloned.1.call-start = ((), (), s32[]{:S(2)}) async-start(), calls=%async_computation.4 | async-start | bytes 6291456 | tf_op jit(solution)/shard_map/reduce_scatter | solution.py:42
  91.9 14.2 %collective-permute-start.2 = (bf16[1,64,16,128]{3,1,2,0:T(8,128)(2,1)S(1)}, bf16[1,64,16,128]{3,1,2,0:T(8,128)(2,1)S(1)}, u32[]{:S(2)}, u32[]{:S(2)}) collective-permute-start(bf16[1,64,16,128]{3,1,2,0:T(8,128)(2,1)S(1)} %get-tuple-element.5), channel_id=1, source_target_pairs={{0,2},{2,4},{4,6},{6,8},{8,10},{10,12},{12,14},{1,3},{3,5},{5,7},{... | collective-permute-start | bytes 786440 | tf_op jit(solution)/shard_map/ppermute | solution.py:14
  95.2 10.8 %collective-permute-start.3 = (bf16[1,64,16,128]{3,1,2,0:T(8,128)(2,1)S(1)}, bf16[1,64,16,128]{3,1,2,0:T(8,128)(2,1)S(1)}, u32[]{:S(2)}, u32[]{:S(2)}) collective-permute-start(bf16[1,64,16,128]{3,1,2,0:T(8,128)(2,1)S(1)} %get-tuple-element.6), channel_id=1, source_target_pairs={{2,0},{4,2},{6,4},{8,6},{10,8},{12,10},{14,12},{3,1},{5,3},{7,5},{... | collective-permute-start | bytes 786440 | tf_op jit(solution)/shard_map/ppermute | solution.py:15
  106.6 2.0 %copy-start.3 = (bf16[3,3,3,256,256]{4,3,2,1,0:T(8,128)(2,1)S(1)}, bf16[3,3,3,256,256]{4,3,2,1,0:T(8,128)(2,1)}, u32[]{:S(2)}) copy-start(bf16[3,3,3,256,256]{4,3,2,1,0:T(8,128)(2,1)} %param.8) | copy-start | bytes 10616836
  126.5 0.7 copy-start.5
  127.2 18.1 %copy-start.1 = (bf16[3,3,3,256,256]{4,3,2,1,0:T(8,128)(2,1)S(1)}, bf16[3,3,3,256,256]{4,3,2,1,0:T(8,128)(2,1)}, u32[]{:S(2)}) copy-start(bf16[3,3,3,256,256]{4,3,2,1,0:T(8,128)(2,1)} %param.6) | copy-start | bytes 10616836
Sparse Core Ops, SparseCore 0:
  73.8 16.0 reduce-scatter.2
  126.6 15.0 reduce-scatter.4
where the time goes:
time: 153 us; the launch traced here: 152 us
  waiting for transfers between devices  44.6 us (29%)
  blocking collectives  31.6 us (21%)
  matrix products  26.9 us (18%)
  local copies, waits for them, and re-layouts  20.4 us (13%)
  between operations  13.6 us (9%)
  starting transfers between devices  9.95 us (7%)
  other arithmetic  5.18 us (3%)
    all_to_all x1, blocking collectives, body(): lax.all_to_all(volume, 'space', split_axis=0, concat_axis=1, tiled=True)  31.6 us
    reduce_scatter x2, waiting for transfers between devices, layer(): lax.psum_scatter(convolve(field, part_kernel), 'chan', scatter_dimension=...  30 us
    conv_general_dilated x2, matrix products, convolve(): lax.conv_general_dilated(field[None], kernel, (1, 1, 1), ((0, 0), (1, 1),...  26.9 us
    ppermute x2, waiting for transfers between devices, padded(): before = lax.ppermute(last, axis, up)  10 us
    conv_general_dilated x6, local copies, waits for them, and re-layouts, convolve(): lax.conv_general_dilated(field[None], kernel, (1, 1, 1), ((0, 0), (1, 1),...  7.73 us
    ppermute x2, starting transfers between devices, padded(): before = lax.ppermute(last, axis, up)  7.16 us
    squeeze x2, local copies, waits for them, and re-layouts, convolve(): lax.conv_general_dilated(field[None], kernel, (1, 1, 1), ((0, 0), (1, 1),...  4.89 us
    ppermute x2, waiting for transfers between devices, padded(): after = lax.ppermute(first, axis, down)  4.54 us
  transfers between devices with their start and end apart: 6, of which 5 were waited for; matrix products, arithmetic and copies ran while one was open for 1% of the time, Pallas kernels for 0%

commit v1 on v0

v1 whole, which is shorter than its diff:
```python
import functools

import jax
import jax.numpy as jnp
from jax import lax
from jax.experimental import pallas as pl
from jax.experimental.pallas import tpu as pltpu
from jax.sharding import PartitionSpec as P

MESH = pl.DeviceIdType.MESH
CHUNK = 2


def kernel(
    slabs, vol, w1_hbm, w2_hbm, bias1, bias2, out,
    xbuf, hid, w1, w2, obuf,
    wsem, lsem, psend, precv, hsend, hrecv, osend, orecv, olocal,
):
    s, c = lax.axis_index("space"), lax.axis_index("chan")
    other = 1 - c
    rows, yb, zc, share = vol.shape
    half = rows // 2
    slab = out.shape[0]
    nb = half // slab
    nq = (half + 4) // CHUNK
    nu = (half + 2) // CHUNK

    def dev(space, chan):
        return {"space": space, "chan": chan}

    load1 = pltpu.make_async_copy(w1_hbm, w1, wsem.at[0])
    load2 = pltpu.make_async_copy(w2_hbm, w2, wsem.at[1])
    load1.start()
    load2.start()

    barrier = pltpu.get_barrier_semaphore()

    def greet(i, carry):
        @pl.when(i != s)
        def _():
            for chan in range(2):
                pl.semaphore_signal(
                    barrier, inc=1, device_id=dev(i, chan), device_id_type=MESH
                )
        return carry

    lax.fori_loop(0, slabs, greet, 0)
    pl.semaphore_signal(barrier, inc=1, device_id=dev(s, other), device_id_type=MESH)

    edge = jnp.zeros((2, 2) + xbuf.shape[2:], xbuf.dtype)

    @pl.when(c == 0)
    def _():
        xbuf[:, 0:2] = edge

    @pl.when(c == 1)
    def _():
        xbuf[:, half + 2 : half + 4] = edge

    side = jnp.zeros((2, half + 4, 2, zc, share), xbuf.dtype)

    @pl.when(s == 0)
    def _():
        xbuf[:, :, 0:2] = side

    @pl.when(s == slabs - 1)
    def _():
        xbuf[:, :, yb + 2 : yb + 4] = side

    pl.semaphore_wait(barrier, 2 * slabs - 1)

    def first_block(space):
        return lax.rem(space + nb // 2, nb)

    def order(k, start, count):
        return jnp.where(start + k < count, start + k, count - 1 - k)

    def valid(q, chan):
        return jnp.where(chan == 0, q >= 1, q <= nq - 2)

    def source(q, chan):
        return pl.ds(chan * half + CHUNK * q - 2, CHUNK)

    def target(q):
        return pl.ds(CHUNK * q, CHUNK)

    def local_in(q):
        return pltpu.make_async_copy(
            vol.at[source(q, c)], xbuf.at[c, target(q), pl.ds(2, yb)], lsem.at[q]
        )

    def partner_in(q):
        return pltpu.make_async_remote_copy(
            src_ref=vol.at[source(q, other)],
            dst_ref=xbuf.at[c, target(q), pl.ds(2, yb)],
            send_sem=psend.at[q],
            recv_sem=precv.at[q],
            device_id=dev(s, other),
            device_id_type=MESH,
        )

    def partner_arrival(q):
        return pltpu.make_async_remote_copy(
            src_ref=xbuf.at[other, target(q), pl.ds(2, yb)],
            dst_ref=xbuf.at[other, target(q), pl.ds(2, yb)],
            send_sem=psend.at[q],
            recv_sem=precv.at[q],
            device_id=dev(s, other),
            device_id_type=MESH,
        )

    def halo_in(q, way, chan):
        return pltpu.make_async_remote_copy(
            src_ref=vol.at[source(q, chan), pl.ds((1 - way) * (yb - 2), 2)],
            dst_ref=xbuf.at[c, target(q), pl.ds(way * (yb + 2), 2)],
            send_sem=hsend.at[way, chan, q],
            recv_sem=hrecv.at[way, c, q],
            device_id=dev(s + 1 - 2 * way, chan),
            device_id_type=MESH,
        )

    def halo_arrival(q, way, chan):
        region = xbuf.at[chan, target(q), pl.ds(way * (yb + 2), 2)]
        return pltpu.make_async_remote_copy(
            src_ref=region,
            dst_ref=region,
            send_sem=hsend.at[way, chan, q],
            recv_sem=hrecv.at[way, chan, q],
            device_id=dev(s, other),
            device_id_type=MESH,
        )

    def has(way):
        return s < slabs - 1 if way == 0 else s > 0

    def send_inputs(k, carry):
        q = order(k, 2 * first_block(s), nq)

        @pl.when(valid(q, c))
        def _():
            local_in(q).start()

        @pl.when(valid(q, other))
        def _():
            partner_in(q).start()

        for way in range(2):
            @pl.when(has(way))
            def _():
                there = order(k, 2 * first_block(s + 1 - 2 * way), nq)
                for chan in range(2):
                    @pl.when(valid(there, chan))
                    def _():
                        halo_in(there, way, chan).start()
        return carry

    lax.fori_loop(0, nq, send_inputs, 0)

    def await_chunk(q):
        @pl.when(valid(q, c))
        def _():
            local_in(q).wait()
            partner_arrival(q).wait_recv()
            for way in range(2):
                @pl.when(has(1 - way))
                def _():
                    for chan in range(2):
                        halo_arrival(q, way, chan).wait_recv()

    def shifted(total, count):
        z = lax.rem(lax.broadcasted_iota(jnp.int32, (count, 1), 0), zc)
        low = jnp.where(z == 0, 0.0, pltpu.roll(total(0), 1, 0))
        high = jnp.where(z == zc - 1, 0.0, pltpu.roll(total(2), count - 1, 0))
        return total(1) + low + high

    def convolve(pieces, weight, bias, count):
        lhs = jnp.concatenate([piece.reshape(count, -1) for piece in pieces], axis=1)
        depth = lhs.shape[1]

        def total(tap):
            rhs = weight[:, :, tap].reshape(depth, weight.shape[-1])
            return jnp.dot(lhs, rhs, preferred_element_type=jnp.float32)

        return jnp.maximum(shifted(total, count) + bias[...], 0.0).astype(jnp.bfloat16)

    def hidden_unit(u):
        r = CHUNK * u
        result = convolve(
            [
                xbuf[h, pl.ds(r + a, CHUNK), b : b + yb + 2]
                for a in range(3)
                for b in range(3)
                for h in range(2)
            ],
            w1, bias1, CHUNK * (yb + 2) * zc,
        )
        hid[pl.ds(r, CHUNK)] = result.reshape(CHUNK, yb + 2, zc, hid.shape[-1])
        line = jnp.zeros((CHUNK, zc, hid.shape[-1]), hid.dtype)

        @pl.when(s == 0)
        def _():
            hid[pl.ds(r, CHUNK), 0] = line

        @pl.when(s == slabs - 1)
        def _():
            hid[pl.ds(r, CHUNK), yb + 1] = line

        plane = jnp.zeros(hid.shape[1:], hid.dtype)

        @pl.when((c == 0) & (u == 0))
        def _():
            hid[0] = plane

        @pl.when((c == 1) & (u == nu - 1))
        def _():
            hid[half + 1] = plane

    start = first_block(s)
    await_chunk(2 * start)
    load1.wait()

    def hidden_step(j):
        u = order(j, 2 * start, nu)
        await_chunk(jnp.where(2 * start + j < nu, u + 1, u))
        hidden_unit(u)

    def out_remote(b, chan):
        return pltpu.make_async_remote_copy(
            src_ref=obuf.at[b, chan],
            dst_ref=out.at[:, pl.ds(yb * s, yb)],
            send_sem=osend.at[b, chan],
            recv_sem=orecv.at[s],
            device_id=dev(nb * c + b, chan),
            device_id_type=MESH,
        )

    def out_local(b):
        return pltpu.make_async_copy(
            obuf.at[b, c], out.at[:, pl.ds(yb * s, yb)], olocal
        )

    def away(b, chan):
        return (nb * c + b != s) | (chan != c)

    def block_step(k, carry):
        lax.fori_loop(
            2 * k + jnp.where(k == 0, 0, 1), 2 * k + 3,
            lambda j, x: (hidden_step(j), x)[1], 0,
        )

        @pl.when(k == 0)
        def _():
            load2.wait()

        b = order(k, start, nb)
        result = convolve(
            [
                hid[pl.ds(slab * b + a, slab), e : e + yb]
                for a in range(3)
                for e in range(3)
            ],
            w2, bias2, slab * yb * zc,
        )
        for chan in range(2):
            obuf[b, chan] = result[:, chan * share : (chan + 1) * share].reshape(
                slab, yb, zc, share
            )
        for chan in range(2):
            @pl.when(away(b, chan))
            def _():
                out_remote(b, chan).start()

        @pl.when(nb * c + b == s)
        def _():
            out_local(b).start()
        return carry

    lax.fori_loop(0, nb, block_step, 0)

    def sent_inputs(q, carry):
        @pl.when(valid(q, other))
        def _():
            partner_in(q).wait_send()

        for way in range(2):
            @pl.when(has(way))
            def _():
                for chan in range(2):
                    @pl.when(valid(q, chan))
                    def _():
                        halo_in(q, way, chan).wait_send()
        return carry

    lax.fori_loop(0, nq, sent_inputs, 0)

    def sent_outputs(b, carry):
        for chan in range(2):
            @pl.when(away(b, chan))
            def _():
                out_remote(b, chan).wait_send()

        @pl.when(nb * c + b == s)
        def _():
            out_local(b).wait()
        return carry

    lax.fori_loop(0, nb, sent_outputs, 0)

    def arrived(i, carry):
        @pl.when((i != s) | (s // nb != c))
        def _():
            region = out.at[:, pl.ds(yb * i, yb)]
            pltpu.make_async_remote_copy(
                src_ref=region,
                dst_ref=region,
                send_sem=osend.at[0, 0],
                recv_sem=orecv.at[i],
                device_id=dev(s, other),
                device_id_type=MESH,
            ).wait_recv()
        return carry

    lax.fori_loop(0, slabs, arrived, 0)


def body(slabs, volume, weight_one, bias_one, weight_two, bias_two):
    rows, yb, zc, share = volume.shape
    half, slab = rows // 2, rows // slabs
    nb = half // slab
    nq = (half + 4) // CHUNK
    channels = weight_one.shape[-1]
    anywhere = pl.BlockSpec(memory_space=pl.ANY)
    vmem = pl.BlockSpec(memory_space=pltpu.VMEM)
    dma = pltpu.SemaphoreType.DMA
    kind = volume.dtype
    return pl.pallas_call(
        functools.partial(kernel, slabs),
        out_shape=jax.ShapeDtypeStruct((slab, yb * slabs, zc, share), kind),
        in_specs=[anywhere, anywhere, anywhere, vmem, vmem],
        out_specs=anywhere,
        scratch_shapes=[
            pltpu.VMEM((2, half + 4, yb + 4, zc, share), kind),
            pltpu.VMEM((half + 2, yb + 2, zc, channels), kind),
            pltpu.VMEM(weight_one.shape, kind),
            pltpu.VMEM(weight_two.shape, kind),
            pltpu.VMEM((nb, 2, slab, yb, zc, share), kind),
            dma((2,)),
            dma((nq,)),
            dma((nq,)),
            dma((nq,)),
            dma((2, 2, nq)),
            dma((2, 2, nq)),
            dma((nb, 2)),
            dma((slabs,)),
            dma,
        ],
        compiler_params=pltpu.CompilerParams(
            collective_id=0, has_side_effects=True, vmem_limit_bytes=58 * 2**20
        ),
    )(volume, weight_one, weight_two, bias_one[None], bias_two[None])


def solution(mesh):
    return jax.shard_map(
        functools.partial(body, mesh.shape["space"]),
        mesh=mesh,
        in_specs=(P(None, "space", "tiles", "chan"), P(), P(), P(), P()),
        out_specs=P("space", None, "tiles", "chan"),
        check_vma=False,
    )
```

time: 153 us -> 50.9 us (0.33)
  Pallas kernels: 0 us -> 48.3 us
  waiting for transfers between devices: 44.6 us -> 0 us
  blocking collectives: 31.6 us -> 0 us
  matrix products: 26.9 us -> 0 us
  local copies, waits for them, and re-layouts: 20.4 us -> 2.38 us
  between operations: 13.6 us -> 0.01 us
  starting transfers between devices: 9.95 us -> 0 us
  other arithmetic: 5.18 us -> 0 us
    pallas_call x0 -> x1, Pallas kernels: none -> 48.3 us  [body(): pl.pallas_call(functools.partial(kernel, slabs), out_shape=jax.ShapeDtype...]
    all_to_all x1 -> x0, blocking collectives: 31.6 us -> none  [body(): lax.all_to_all(volume, 'space', split_axis=0, concat_axis=1, tiled=True)]
    reduce_scatter x2 -> x0, waiting for transfers between devices: 30 us -> none  [layer(): lax.psum_scatter(convolve(field, part_kernel), 'chan', scatter_dimension=...]
    conv_general_dilated x2 -> x0, matrix products: 26.9 us -> none  [convolve(): lax.conv_general_dilated(field[None], kernel, (1, 1, 1), ((0, 0), (1, 1),...]
    ppermute x4 -> x0, waiting for transfers between devices: 14.5 us -> none  [the longest x2 10 us: padded(): before = lax.ppermute(last, axis, up)]
    ppermute x4 -> x0, starting transfers between devices: 9.91 us -> none  [the longest x2 7.16 us: padded(): before = lax.ppermute(last, axis, up)]
    conv_general_dilated x6 -> x0, local copies, waits for them, and re-layouts: 7.73 us -> none  [convolve(): lax.conv_general_dilated(field[None], kernel, (1, 1, 1), ((0, 0), (1, 1),...]
    squeeze x2 -> x0, local copies, waits for them, and re-layouts: 4.89 us -> none  [convolve(): lax.conv_general_dilated(field[None], kernel, (1, 1, 1), ((0, 0), (1, 1),...]
  transfers between devices with their start and end apart: 6 -> 0, of which waited for: 5 -> 0; matrix products, arithmetic and copies ran while one was open for 1% -> 0% of each run, Pallas kernels for 0% -> 0%
where the time goes in v1:
time: 50.9 us; the launch traced here: 50.6 us
  Pallas kernels  48.3 us (95%)
  local copies, waits for them, and re-layouts  2.38 us (5%)
    pallas_call x1, Pallas kernels, body(): pl.pallas_call(functools.partial(kernel, slabs), out_shape=jax.ShapeDtype...  48.3 us
    unnamed x1, local copies, waits for them, and re-layouts  2.38 us

profile of v1, /device:TPU:1, one launch (start us, length us, event | category | flops | bytes accessed | tf_op | source)
XLA Modules:
  0.0 50.6 jit_solution(18146319242604117456)
XLA Ops:
  0.0 48.3 %shard_map.55 = bf16[4,64,16,128]{3,2,1,0:T(8,128)(2,1)} custom-call(bf16[32,8,16,128]{3,2,1,0:T(8,128)(2,1)} %vol.1, bf16[3,3,3,256,256]{4,3,2,1,0:T(8,128)(2,1)} %w1_hbm.1, bf16[3,3,3,256,256]{4,3,2,1,0:T(8,128)(2,1)} %w2_hbm.1, f32[1,256]{1,0:T(1,128)} %bitcast.2, f32[1,256]{1,0:T(1,128)} %bitcast.3), custom_call_target="tpu_custom_call" | custom-call | tf_op jit(solution)/shard_map/pallas_call | solution.py:336
  48.3 2.4 %copy.7 = bf16[4,64,16,128]{3,2,1,0:T(8,128)(2,1)} copy(bf16[4,64,16,128]{3,2,1,0:T(8,128)(2,1)} %shard_map.55) | data formatting | bytes 2097152

commit v2 on v1

--- a/solution.py
+++ b/solution.py
@@ -70,7 +70,7 @@
     pl.semaphore_wait(barrier, 2 * slabs - 1)
 
     def first_block(space):
-        return lax.rem(space + nb // 2, nb)
+        return lax.rem(space // 2 + nb // 2 + lax.rem(space, 2) * (nb // 2), nb)
 
     def order(k, start, count):
         return jnp.where(start + k < count, start + k, count - 1 - k)
@@ -154,7 +154,7 @@
                         halo_in(there, way, chan).start()
         return carry
 
-    lax.fori_loop(0, nq, send_inputs, 0)
+    lax.fori_loop(0, 5, send_inputs, 0)
 
     def await_chunk(q):
         @pl.when(valid(q, c))
@@ -220,6 +220,10 @@
     load1.wait()
 
     def hidden_step(j):
+        @pl.when(j + 5 < nq)
+        def _():
+            send_inputs(j + 5, 0)
+
         u = order(j, 2 * start, nu)
         await_chunk(jnp.where(2 * start + j < nu, u + 1, u))
         hidden_unit(u)

time: 50.9 us -> 49.4 us (0.971)
  Pallas kernels: 48.3 us -> 46.8 us
    pallas_call x1, Pallas kernels: 48.3 us -> 46.8 us  [body(): pl.pallas_call(functools.partial(kernel, slabs), out_shape=jax.ShapeDtype...]
where the time goes in v2:
time: 49.4 us; the launch traced here: 49.2 us
  Pallas kernels  46.8 us (95%)
  local copies, waits for them, and re-layouts  2.38 us (5%)
    pallas_call x1, Pallas kernels, body(): pl.pallas_call(functools.partial(kernel, slabs), out_shape=jax.ShapeDtype...  46.8 us
    unnamed x1, local copies, waits for them, and re-layouts  2.38 us

profile of v2, /device:TPU:1, one launch (start us, length us, event | category | flops | bytes accessed | tf_op | source)
XLA Modules:
  0.0 49.2 jit_solution(13693139410835849445)
XLA Ops:
  0.0 46.8 %shard_map.55 = bf16[4,64,16,128]{3,2,1,0:T(8,128)(2,1)} custom-call(bf16[32,8,16,128]{3,2,1,0:T(8,128)(2,1)} %vol.1, bf16[3,3,3,256,256]{4,3,2,1,0:T(8,128)(2,1)} %w1_hbm.1, bf16[3,3,3,256,256]{4,3,2,1,0:T(8,128)(2,1)} %w2_hbm.1, f32[1,256]{1,0:T(1,128)} %bitcast.2, f32[1,256]{1,0:T(1,128)} %bitcast.3), custom_call_target="tpu_custom_call" | custom-call | tf_op jit(solution)/shard_map/pallas_call | solution.py:340
  46.8 2.4 %copy.7 = bf16[4,64,16,128]{3,2,1,0:T(8,128)(2,1)} copy(bf16[4,64,16,128]{3,2,1,0:T(8,128)(2,1)} %shard_map.55) | data formatting | bytes 2097152

commit v3 on v2

--- a/solution.py
+++ b/solution.py
@@ -70,7 +70,7 @@
     pl.semaphore_wait(barrier, 2 * slabs - 1)
 
     def first_block(space):
-        return lax.rem(space // 2 + nb // 2 + lax.rem(space, 2) * (nb // 2), nb)
+        return lax.rem(space // 2 + nb // 2 + lax.rem(space, 2), nb)
 
     def order(k, start, count):
         return jnp.where(start + k < count, start + k, count - 1 - k)

time: 49.4 us -> 47.1 us (0.953)
  Pallas kernels: 46.8 us -> 44.5 us
    pallas_call x1, Pallas kernels: 46.8 us -> 44.5 us  [body(): pl.pallas_call(functools.partial(kernel, slabs), out_shape=jax.ShapeDtype...]
where the time goes in v3:
time: 47.1 us; the launch traced here: 46.9 us
  Pallas kernels  44.5 us (94%)
  local copies, waits for them, and re-layouts  2.38 us (5%)
    pallas_call x1, Pallas kernels, body(): pl.pallas_call(functools.partial(kernel, slabs), out_shape=jax.ShapeDtype...  44.5 us
    unnamed x1, local copies, waits for them, and re-layouts  2.38 us

profile of v3, /device:TPU:1, one launch (start us, length us, event | category | flops | bytes accessed | tf_op | source)
XLA Modules:
  0.0 46.9 jit_solution(15992521461937734019)
XLA Ops:
  0.0 44.5 %shard_map.55 = bf16[4,64,16,128]{3,2,1,0:T(8,128)(2,1)} custom-call(bf16[32,8,16,128]{3,2,1,0:T(8,128)(2,1)} %vol.1, bf16[3,3,3,256,256]{4,3,2,1,0:T(8,128)(2,1)} %w1_hbm.1, bf16[3,3,3,256,256]{4,3,2,1,0:T(8,128)(2,1)} %w2_hbm.1, f32[1,256]{1,0:T(1,128)} %bitcast.2, f32[1,256]{1,0:T(1,128)} %bitcast.3), custom_call_target="tpu_custom_call" | custom-call | tf_op jit(solution)/shard_map/pallas_call | solution.py:340
  44.5 2.4 %copy.7 = bf16[4,64,16,128]{3,2,1,0:T(8,128)(2,1)} copy(bf16[4,64,16,128]{3,2,1,0:T(8,128)(2,1)} %shard_map.55) | data formatting | bytes 2097152
